TPU v7x, 128 devices: a whole 4x4x4 slice. The times are simulated.
128 devices in a mesh: dp: 2 (over core), blk: 32 (over z_hi, x, y), head: 2 (over z_lo).
Axes of the slice: x: 4, y: 4, z: 4 (z_hi: 2, z_lo: 2; z = z_hi * 2 + z_lo), core: 2. Of those that a mesh axis runs over, the one named last changes fastest.
Arguments:
- stored_query_rows: bfloat16 [16384, 8192], P(('dp', 'blk', 'head')), parts along dimension 0
- stored_key_rows: bfloat16 [16384, 1024], P(('dp', 'blk', 'head')), parts along dimension 0
- stored_value_rows: bfloat16 [16384, 1024], P(('dp', 'blk', 'head')), parts along dimension 0, may hold values from -6 to 6
- block_docs: int32 [128], P('dp'), parts along dimension 0, may hold values from 0 to 15, never falling along the last dimension, each value on 1 to 8 neighbouring positions
Outputs:
- context: bfloat16 [16384, 8192], P(('dp', 'blk', 'head')), parts along dimension 0
There are 2 independent parts, one for each index of `dp`. A program takes and returns all parts, laid end to end along the dimension named above; each array names one. Nothing has to cross between parts.
Inputs may be any that keep to these rules, and one draw needn't show every extreme that they name: `block_docs`: document numbers never fall along the sequence; each document covers 1 to 8 blocks, and one covers exactly 8.
All inputs are finite; a program needn't handle non-finite values.
Results may differ from a plain program's by a relative error of at most 0.0045.
Values may be sent and summed in bfloat16 or wider, within the bound.
A program may use at most 128 MiB of HBM per device.

v0:
```python
import math

import jax
import jax.numpy as jnp
from jax import lax
from jax.sharding import PartitionSpec as P

HEAD_DIMENSION = 128
MASK_BLOCK_SIZE = 128


def from_behind(x, axis, by):
    length = lax.axis_size(axis)
    pairs = [(i, i + by) for i in range(length) if 0 <= i + by < length]
    return lax.ppermute(x, axis, pairs)


def on_device(stored_query_rows, stored_key_rows, stored_value_rows, block_docs):
    piece_rows = stored_query_rows.shape[0]
    blk_count = lax.axis_size("blk")
    my_index = lax.axis_index("blk")
    query_all, key_all, value_all = (
        lax.all_to_all(stored_query_rows, "head", split_axis=1, concat_axis=0, tiled=True),
        lax.all_to_all(stored_key_rows, "head", split_axis=1, concat_axis=0, tiled=True),
        lax.all_to_all(stored_value_rows, "head", split_axis=1, concat_axis=0, tiled=True),
    )
    kv_heads = key_all.shape[1] // HEAD_DIMENSION
    q_heads = query_all.shape[1] // HEAD_DIMENSION
    query_group = q_heads // kv_heads
    per_piece = piece_rows // MASK_BLOCK_SIZE
    local_blocks = 2 * per_piece
    scale = 1.0 / math.sqrt(HEAD_DIMENSION)
    offsets = jnp.arange(MASK_BLOCK_SIZE, dtype=jnp.int32)

    def block_place(holder, within):
        piece_index = jnp.where(within < per_piece, holder, 2 * blk_count - 1 - holder)
        global_block = piece_index * per_piece + within % per_piece
        safe_block = jnp.clip(global_block, 0, block_docs.shape[0] - 1)
        return (global_block, lax.dynamic_index_in_dim(block_docs, safe_block, keepdims=False))

    query_blocks = []
    query_places = []
    for qblock in range(local_blocks):
        query_blocks.append(
            query_all[qblock * MASK_BLOCK_SIZE : (qblock + 1) * MASK_BLOCK_SIZE].reshape(
                MASK_BLOCK_SIZE, kv_heads, query_group, HEAD_DIMENSION
            )
        )
        query_places.append(block_place(my_index, qblock))

    def absorb(carry, key_block, value_block, key_global, key_doc, valid):
        key_pos = key_global * MASK_BLOCK_SIZE + offsets
        key_three = key_block.reshape(MASK_BLOCK_SIZE, kv_heads, HEAD_DIMENSION)
        value_three = value_block.reshape(MASK_BLOCK_SIZE, kv_heads, HEAD_DIMENSION)
        updated = []
        for qblock in range(local_blocks):
            query_global, query_doc = query_places[qblock]
            query_pos = query_global * MASK_BLOCK_SIZE + offsets
            needed = valid & (key_doc == query_doc) & (key_global <= query_global)

            def take(state, qblock=qblock, query_pos=query_pos):
                running, total, summed = state
                score = (
                    jnp.einsum(
                        "qhgd,khd->hgqk",
                        query_blocks[qblock],
                        key_three,
                        preferred_element_type=jnp.float32,
                    )
                    * scale
                )
                allowed = key_pos[None, :] <= query_pos[:, None]
                score = jnp.where(allowed, score, -1e30)
                newtop = jnp.maximum(running, jnp.max(score, axis=-1))
                factor = jnp.exp(running - newtop)
                weight = jnp.where(allowed, jnp.exp(score - newtop[..., None]), 0.0)
                total = total * factor + jnp.sum(weight, axis=-1)
                product = jnp.einsum(
                    "hgqk,khd->qhgd",
                    weight.astype(jnp.bfloat16),
                    value_three,
                    preferred_element_type=jnp.float32,
                )
                summed = summed * jnp.moveaxis(factor, 2, 0)[..., None] + product
                return (newtop, total, summed)

            updated.append(lax.cond(needed, take, lambda state: state, carry[qblock]))
        return tuple(updated)

    def fold_keys(carry, piece, first_token, valid):
        count = piece.shape[1] // MASK_BLOCK_SIZE
        key_stack = piece[0].reshape(count, MASK_BLOCK_SIZE, piece.shape[2])
        value_stack = piece[1].reshape(count, MASK_BLOCK_SIZE, piece.shape[2])

        def one_step(state, inputs):
            key_block, value_block, number = inputs
            stored_block = first_token // MASK_BLOCK_SIZE + number
            global_block, doc_value = block_place(
                stored_block // local_blocks, stored_block % local_blocks
            )
            return (absorb(state, key_block, value_block, global_block, doc_value, valid), None)

        result, unused = lax.scan(
            one_step, carry, (key_stack, value_stack, jnp.arange(count, dtype=jnp.int32))
        )
        return result

    empty = tuple(
        (
            (
                jnp.full((kv_heads, query_group, MASK_BLOCK_SIZE), -1e30, jnp.float32),
                jnp.zeros((kv_heads, query_group, MASK_BLOCK_SIZE), jnp.float32),
                jnp.zeros((MASK_BLOCK_SIZE, kv_heads, query_group, HEAD_DIMENSION), jnp.float32),
            )
            for qblock in range(local_blocks)
        )
    )
    stacked = jnp.stack([key_all, value_all])
    reach = blk_count // 4
    carry = fold_keys(empty, stacked, my_index * 2 * piece_rows, jnp.bool_(True))
    for distance in range(1, reach + 1):
        lower = from_behind(stacked, "blk", distance)
        carry = fold_keys(
            carry, lower, (my_index - distance) * 2 * piece_rows, my_index - distance >= 0
        )
        upper = from_behind(stacked, "blk", -distance)
        carry = fold_keys(
            carry, upper, (my_index + distance) * 2 * piece_rows, my_index + distance < blk_count
        )
    pieces = []
    for qblock in range(local_blocks):
        running, total, summed = carry[qblock]
        normed = summed / jnp.moveaxis(total, 2, 0)[..., None]
        pieces.append(
            normed.reshape(MASK_BLOCK_SIZE, q_heads * HEAD_DIMENSION).astype(jnp.bfloat16)
        )
    attended = jnp.concatenate(pieces, axis=0)
    return lax.all_to_all(attended, "head", split_axis=0, concat_axis=1, tiled=True)


def solution(mesh):
    placed = (
        P(("dp", "blk", "head"), None),
        P(("dp", "blk", "head"), None),
        P(("dp", "blk", "head"), None),
        P("dp"),
    )
    return jax.shard_map(
        on_device,
        mesh=mesh,
        in_specs=placed,
        out_specs=P(("dp", "blk", "head"), None),
        check_vma=False,
    )
```

profile of v0, /device:TPU:3, one launch (start us, length us, event | category | flops | bytes accessed | tf_op | source)
XLA Modules:
  0.0 515.4 jit_solution(12130635575063531723)
XLA Ops:
  57.3 13.4 %collective-permute-done.3 = bf16[2,256,512]{2,1,0:T(8,128)(2,1)S(1)} collective-permute-done((bf16[2,256,512]{2,1,0:T(8,128)(2,1)}, bf16[2,256,512]{2,1,0:T(8,128)(2,1)S(1)}, u32[]{:S(2)}, u32[]{:S(2)}) %collective-permute-start.3) | collective-permute-done | bytes 524320 | tf_op jit(solution)/shard_map/ppermute | solution.py:15
  78.8 7.4 %collective-permute-start.10 = (bf16[2,256,512]{2,1,0:T(8,128)(2,1)}, bf16[2,256,512]{2,1,0:T(8,128)(2,1)S(1)}, u32[]{:S(2)}, u32[]{:S(2)}) collective-permute-start(bf16[2,256,512]{2,1,0:T(8,128)(2,1)} %pad_maximum_fusion.1), channel_id=1, source_target_pairs={{0,12},{2,14},{4,16},{6,18},{8,20},{10,22},{12,24},{14,26},{16,28}... | collective-permute-start | bytes 1572872 | tf_op jit(solution)/shard_map/ppermute | solution.py:15
  89.1 6.9 %collective-permute-start.12 = (bf16[2,256,512]{2,1,0:T(8,128)(2,1)}, bf16[2,256,512]{2,1,0:T(8,128)(2,1)S(1)}, u32[]{:S(2)}, u32[]{:S(2)}) collective-permute-start(bf16[2,256,512]{2,1,0:T(8,128)(2,1)} %pad_maximum_fusion.1), channel_id=1, source_target_pairs={{0,14},{2,16},{4,18},{6,20},{8,22},{10,24},{12,26},{14,28},{16,30}... | collective-permute-start | bytes 1572872 | tf_op jit(solution)/shard_map/ppermute | solution.py:15
  99.1 7.4 %collective-permute-start.14 = (bf16[2,256,512]{2,1,0:T(8,128)(2,1)}, bf16[2,256,512]{2,1,0:T(8,128)(2,1)S(1)}, u32[]{:S(2)}, u32[]{:S(2)}) collective-permute-start(bf16[2,256,512]{2,1,0:T(8,128)(2,1)} %pad_maximum_fusion.1), channel_id=1, source_target_pairs={{0,16},{2,18},{4,20},{6,22},{8,24},{10,26},{12,28},{14,30},{16,32}... | collective-permute-start | bytes 1572872 | tf_op jit(solution)/shard_map/ppermute | solution.py:15
  109.6 8.9 %collective-permute-done.11 = bf16[2,256,512]{2,1,0:T(8,128)(2,1)S(1)} collective-permute-done((bf16[2,256,512]{2,1,0:T(8,128)(2,1)}, bf16[2,256,512]{2,1,0:T(8,128)(2,1)S(1)}, u32[]{:S(2)}, u32[]{:S(2)}) %collective-permute-start.11) | collective-permute-done | bytes 524320 | tf_op jit(solution)/shard_map/ppermute | solution.py:15
  120.1 32.5 %collective-permute-done.13 = bf16[2,256,512]{2,1,0:T(8,128)(2,1)S(1)} collective-permute-done((bf16[2,256,512]{2,1,0:T(8,128)(2,1)}, bf16[2,256,512]{2,1,0:T(8,128)(2,1)S(1)}, u32[]{:S(2)}, u32[]{:S(2)}) %collective-permute-start.13) | collective-permute-done | bytes 524320 | tf_op jit(solution)/shard_map/ppermute | solution.py:15
  161.0 18.9 %while.425 = (s32[]{:T(128)}, f32[4,8,128]{2,1,0:T(8,128)S(1)}, f32[4,8,128]{2,1,0:T(8,128)S(1)}, f32[128,4,8,128]{3,0,2,1:T(8,128)S(1)}, f32[4,8,128]{2,1,0:T(8...) while((s32[]{:T(128)}, f32[4,8,128]{2,1,0:T(8,128)S(1)}, ...), condition=%wide.region_9.10_spmd.clone.clone, body=%wide.region_0.9_spmd.clone.clone.sunk | while | flops 552657280 | bytes 24778572 | solution.py:103
  180.0 17.2 %while.426 = (s32[]{:T(128)}, f32[4,8,128]{2,1,0:T(8,128)S(1)}, f32[4,8,128]{2,1,0:T(8,128)S(1)}, f32[128,4,8,128]{3,0,2,1:T(8,128)S(1)}, f32[4,8,128]{2,1,0:T(8...) while((s32[]{:T(128)}, f32[4,8,128]{2,1,0:T(8,128)S(1)}, ...), condition=%wide.region_19.20_spmd.clone.clone, body=%wide.region_10.19_spmd.clone.clone.sunk | while | flops 552657280 | bytes 25302876 | solution.py:103
  197.2 20.2 %while.427 = (s32[]{:T(128)}, f32[4,8,128]{2,1,0:T(8,128)S(1)}, f32[4,8,128]{2,1,0:T(8,128)S(1)}, f32[128,4,8,128]{3,0,2,1:T(8,128)S(1)}, f32[4,8,128]{2,1,0:T(8...) while((s32[]{:T(128)}, f32[4,8,128]{2,1,0:T(8,128)S(1)}, ...), condition=%wide.region_29.30_spmd.clone.clone, body=%wide.region_20.29_spmd.clone.clone.sunk | while | flops 552657280 | bytes 25302876 | solution.py:103
  217.5 17.5 %while.428 = (s32[]{:T(128)}, f32[4,8,128]{2,1,0:T(8,128)S(1)}, f32[4,8,128]{2,1,0:T(8,128)S(1)}, f32[128,4,8,128]{3,0,2,1:T(8,128)S(1)}, f32[4,8,128]{2,1,0:T(8...) while((s32[]{:T(128)}, f32[4,8,128]{2,1,0:T(8,128)S(1)}, ...), condition=%wide.region_39.40_spmd.clone.clone, body=%wide.region_30.39_spmd.clone.clone.sunk | while | flops 552657280 | bytes 25302876 | solution.py:103
  235.0 20.9 %while.429 = (s32[]{:T(128)}, f32[4,8,128]{2,1,0:T(8,128)S(1)}, f32[4,8,128]{2,1,0:T(8,128)S(1)}, f32[128,4,8,128]{3,0,2,1:T(8,128)S(1)}, f32[4,8,128]{2,1,0:T(8...) while((s32[]{:T(128)}, f32[4,8,128]{2,1,0:T(8,128)S(1)}, ...), condition=%wide.region_49.50_spmd.clone.clone, body=%wide.region_40.49_spmd.clone.clone.sunk | while | flops 552657280 | bytes 25302876 | solution.py:103
  255.9 17.4 %while.430 = (s32[]{:T(128)}, f32[4,8,128]{2,1,0:T(8,128)S(1)}, f32[4,8,128]{2,1,0:T(8,128)S(1)}, f32[128,4,8,128]{3,0,2,1:T(8,128)S(1)}, f32[4,8,128]{2,1,0:T(8...) while((s32[]{:T(128)}, f32[4,8,128]{2,1,0:T(8,128)S(1)}, ...), condition=%wide.region_59.60_spmd.clone.clone, body=%wide.region_50.59_spmd.clone.clone.sunk | while | flops 552657280 | bytes 25302876 | solution.py:103
  273.3 14.3 %while.431 = (s32[]{:T(128)}, f32[4,8,128]{2,1,0:T(8,128)S(1)}, f32[4,8,128]{2,1,0:T(8,128)S(1)}, f32[128,4,8,128]{3,0,2,1:T(8,128)S(1)}, f32[4,8,128]{2,1,0:T(8...) while((s32[]{:T(128)}, f32[4,8,128]{2,1,0:T(8,128)S(1)}, ...), condition=%wide.region_69.70_spmd.clone.clone, body=%wide.region_60.69_spmd.clone.clone.sunk | while | flops 552657280 | bytes 25302876 | solution.py:103
  287.6 17.2 %while.432 = (s32[]{:T(128)}, f32[4,8,128]{2,1,0:T(8,128)S(1)}, f32[4,8,128]{2,1,0:T(8,128)S(1)}, f32[128,4,8,128]{3,0,2,1:T(8,128)S(1)}, f32[4,8,128]{2,1,0:T(8...) while((s32[]{:T(128)}, f32[4,8,128]{2,1,0:T(8,128)S(1)}, ...), condition=%wide.region_79.80_spmd.clone.clone, body=%wide.region_70.79_spmd.clone.clone.sunk | while | flops 552657280 | bytes 25302876 | solution.py:103
  304.8 14.8 %while.433 = (s32[]{:T(128)}, f32[4,8,128]{2,1,0:T(8,128)S(1)}, f32[4,8,128]{2,1,0:T(8,128)S(1)}, f32[128,4,8,128]{3,0,2,1:T(8,128)S(1)}, f32[4,8,128]{2,1,0:T(8...) while((s32[]{:T(128)}, f32[4,8,128]{2,1,0:T(8,128)S(1)}, ...), condition=%wide.region_89.90_spmd.clone.clone, body=%wide.region_80.89_spmd.clone.clone.sunk | while | flops 552657280 | bytes 25302876 | solution.py:103
  319.6 14.2 %while.434 = (s32[]{:T(128)}, f32[4,8,128]{2,1,0:T(8,128)S(1)}, f32[4,8,128]{2,1,0:T(8,128)S(1)}, f32[128,4,8,128]{3,0,2,1:T(8,128)S(1)}, f32[4,8,128]{2,1,0:T(8...) while((s32[]{:T(128)}, f32[4,8,128]{2,1,0:T(8,128)S(1)}, ...), condition=%wide.region_99.100_spmd.clone.clone, body=%wide.region_90.99_spmd.clone.clone.sunk | while | flops 552657280 | bytes 25302876 | solution.py:103
  333.8 15.1 %while.435 = (s32[]{:T(128)}, f32[4,8,128]{2,1,0:T(8,128)S(1)}, f32[4,8,128]{2,1,0:T(8,128)S(1)}, f32[128,4,8,128]{3,0,2,1:T(8,128)S(1)}, f32[4,8,128]{2,1,0:T(8...) while((s32[]{:T(128)}, f32[4,8,128]{2,1,0:T(8,128)S(1)}, ...), condition=%wide.region_109.110_spmd.clone.clone, body=%wide.region_100.109_spmd.clone.clone.sunk | while | flops 552657280 | bytes 25302876 | solution.py:103
  348.9 15.3 %while.436 = (s32[]{:T(128)}, f32[4,8,128]{2,1,0:T(8,128)S(1)}, f32[4,8,128]{2,1,0:T(8,128)S(1)}, f32[128,4,8,128]{3,0,2,1:T(8,128)S(1)}, f32[4,8,128]{2,1,0:T(8...) while((s32[]{:T(128)}, f32[4,8,128]{2,1,0:T(8,128)S(1)}, ...), condition=%wide.region_119.120_spmd.clone.clone, body=%wide.region_110.119_spmd.clone.clone.sunk | while | flops 552657280 | bytes 25302876 | solution.py:103
  364.2 15.4 %while.437 = (s32[]{:T(128)}, f32[4,8,128]{2,1,0:T(8,128)S(1)}, f32[4,8,128]{2,1,0:T(8,128)S(1)}, f32[128,4,8,128]{3,0,2,1:T(8,128)S(1)}, f32[4,8,128]{2,1,0:T(8...) while((s32[]{:T(128)}, f32[4,8,128]{2,1,0:T(8,128)S(1)}, ...), condition=%wide.region_129.130_spmd.clone.clone, body=%wide.region_120.129_spmd.clone.clone.sunk | while | flops 552657280 | bytes 25302876 | solution.py:103
  379.6 13.9 %while.438 = (s32[]{:T(128)}, f32[4,8,128]{2,1,0:T(8,128)S(1)}, f32[4,8,128]{2,1,0:T(8,128)S(1)}, f32[128,4,8,128]{3,0,2,1:T(8,128)S(1)}, f32[4,8,128]{2,1,0:T(8...) while((s32[]{:T(128)}, f32[4,8,128]{2,1,0:T(8,128)S(1)}, ...), condition=%wide.region_139.140_spmd.clone.clone, body=%wide.region_130.139_spmd.clone.clone.sunk | while | flops 552657280 | bytes 25302876 | solution.py:103
  393.5 14.9 %while.439 = (s32[]{:T(128)}, f32[4,8,128]{2,1,0:T(8,128)S(1)}, f32[4,8,128]{2,1,0:T(8,128)S(1)}, f32[128,4,8,128]{3,0,2,1:T(8,128)S(1)}, f32[4,8,128]{2,1,0:T(8...) while((s32[]{:T(128)}, f32[4,8,128]{2,1,0:T(8,128)S(1)}, ...), condition=%wide.region_149.150_spmd.clone.clone, body=%wide.region_140.149_spmd.clone.clone.sunk | while | flops 552657280 | bytes 25302876 | solution.py:103
  408.5 14.1 %while.440 = (s32[]{:T(128)}, f32[4,8,128]{2,1,0:T(8,128)S(1)}, f32[4,8,128]{2,1,0:T(8,128)S(1)}, f32[128,4,8,128]{3,0,2,1:T(8,128)S(1)}, f32[4,8,128]{2,1,0:T(8...) while((s32[]{:T(128)}, f32[4,8,128]{2,1,0:T(8,128)S(1)}, ...), condition=%wide.region_159.160_spmd.clone.clone, body=%wide.region_150.159_spmd.clone.clone.sunk | while | flops 552657280 | bytes 25302876 | solution.py:103
  422.6 14.2 %while.441 = (s32[]{:T(128)}, f32[4,8,128]{2,1,0:T(8,128)S(1)}, f32[4,8,128]{2,1,0:T(8,128)S(1)}, f32[128,4,8,128]{3,0,2,1:T(8,128)S(1)}, f32[4,8,128]{2,1,0:T(8...) while((s32[]{:T(128)}, f32[4,8,128]{2,1,0:T(8,128)S(1)}, ...), condition=%wide.region_169.170_spmd.clone.clone, body=%wide.region_160.169_spmd.clone.clone.sunk | while | flops 552657280 | bytes 25302876 | solution.py:103
  445.8 62.8 %all_to_all.67 = bf16[2,128,4096]{2,1,0:T(8,128)(2,1)S(1)} all-to-all(bf16[2,128,4096]{2,1,0:T(8,128)(2,1)} %bitcast.1279), channel_id=1, replica_groups=mesh['dp'=2,'blk'=32,'head'=2] {'head'}, dimensions={0} | all-to-all | bytes 4194304 | tf_op jit(solution)/shard_map/all_to_all | solution.py:138
  (463 shorter events, 294.9 us)
Async XLA Ops:
  0.0 28.9 %copy-start.2 = (bf16[128,8192]{1,0:T(8,128)(2,1)S(1)}, bf16[128,8192]{1,0:T(8,128)(2,1)}, u32[]{:S(2)}) copy-start(bf16[128,8192]{1,0:T(8,128)(2,1)} %param.106) | copy-start | bytes 6291460
  1.9 8.4 %all-to-all-start = ((bf16[128,2,512]{0,2,1:T(8,128)(2,1)}), bf16[128,2,512]{0,2,1:T(8,128)(2,1)S(1)}, u32[]{:S(2)}, u32[]{:S(2)}) async-start(bf16[128,2,512]{0,2,1:T(8,128)(2,1)} %bitcast.171), calls=%async_computation | async-start | bytes 524288 | tf_op jit(solution)/shard_map/all_to_all | solution.py:24
  10.3 21.0 %copy-start = (bf16[128,2,512]{0,2,1:T(8,128)(2,1)}, bf16[128,2,512]{0,2,1:T(8,128)(2,1)S(1)}, u32[]{:S(2)}) copy-start(bf16[128,2,512]{0,2,1:T(8,128)(2,1)S(1)} %all-to-all-done) | copy-start | bytes 786436
  10.3 7.5 %all-to-all-start.1 = ((bf16[128,2,512]{0,2,1:T(8,128)(2,1)}), bf16[128,2,512]{0,2,1:T(8,128)(2,1)S(1)}, u32[]{:S(2)}, u32[]{:S(2)}) async-start(bf16[128,2,512]{0,2,1:T(8,128)(2,1)} %bitcast.173), calls=%async_computation.1 | async-start | bytes 524288 | tf_op jit(solution)/shard_map/all_to_all | solution.py:25
  17.8 13.6 %copy-start.1 = (bf16[128,2,512]{0,2,1:T(8,128)(2,1)}, bf16[128,2,512]{0,2,1:T(8,128)(2,1)S(1)}, u32[]{:S(2)}) copy-start(bf16[128,2,512]{0,2,1:T(8,128)(2,1)S(1)} %all-to-all-done.1) | copy-start | bytes 786436
  18.8 24.3 %collective-permute-start = (bf16[2,256,512]{2,1,0:T(8,128)(2,1)}, bf16[2,256,512]{2,1,0:T(8,128)(2,1)}, u32[]{:S(2)}, u32[]{:S(2)}) collective-permute-start(bf16[2,256,512]{2,1,0:T(8,128)(2,1)} %pad_maximum_fusion.1), channel_id=1, source_target_pairs={{0,2},{2,4},{4,6},{6,8},{8,10},{10,12},{12,14},{14,16},{16,18},{18... | collective-permute-start | bytes 1572872 | tf_op jit(solution)/shard_map/ppermute | solution.py:15
  22.0 27.3 %collective-permute-start.1 = (bf16[2,256,512]{2,1,0:T(8,128)(2,1)}, bf16[2,256,512]{2,1,0:T(8,128)(2,1)}, u32[]{:S(2)}, u32[]{:S(2)}) collective-permute-start(bf16[2,256,512]{2,1,0:T(8,128)(2,1)} %pad_maximum_fusion.1), channel_id=1, source_target_pairs={{2,0},{4,2},{6,4},{8,6},{10,8},{12,10},{14,12},{16,14},{18,16},{20... | collective-permute-start | bytes 1572872 | tf_op jit(solution)/shard_map/ppermute | solution.py:15
  26.2 28.1 %collective-permute-start.2 = (bf16[2,256,512]{2,1,0:T(8,128)(2,1)}, bf16[2,256,512]{2,1,0:T(8,128)(2,1)S(1)}, u32[]{:S(2)}, u32[]{:S(2)}) collective-permute-start(bf16[2,256,512]{2,1,0:T(8,128)(2,1)} %pad_maximum_fusion.1), channel_id=1, source_target_pairs={{0,4},{2,6},{4,8},{6,10},{8,12},{10,14},{12,16},{14,18},{16,20},{1... | collective-permute-start | bytes 1572872 | tf_op jit(solution)/shard_map/ppermute | solution.py:15
  31.4 4.2 copy-start.3
  31.4 123.8 %all-to-all-start.2 = ((bf16[128,2,4096]{0,2,1:T(8,128)(2,1)}), bf16[128,2,4096]{0,2,1:T(8,128)(2,1)S(1)}, u32[]{:S(2)}, u32[]{:S(2)}) async-start(bf16[128,2,4096]{0,2,1:T(8,128)(2,1)} %bitcast.1278), calls=%async_computation.2 | async-start | bytes 4194304 | tf_op jit(solution)/shard_map/all_to_all | solution.py:23
  36.2 34.5 %collective-permute-start.3 = (bf16[2,256,512]{2,1,0:T(8,128)(2,1)}, bf16[2,256,512]{2,1,0:T(8,128)(2,1)S(1)}, u32[]{:S(2)}, u32[]{:S(2)}) collective-permute-start(bf16[2,256,512]{2,1,0:T(8,128)(2,1)} %pad_maximum_fusion.1), channel_id=1, source_target_pairs={{4,0},{6,2},{8,4},{10,6},{12,8},{14,10},{16,12},{18,14},{20,16},{2... | collective-permute-start | bytes 1572872 | tf_op jit(solution)/shard_map/ppermute | solution.py:15
  41.2 35.5 %collective-permute-start.4 = (bf16[2,256,512]{2,1,0:T(8,128)(2,1)}, bf16[2,256,512]{2,1,0:T(8,128)(2,1)S(1)}, u32[]{:S(2)}, u32[]{:S(2)}) collective-permute-start(bf16[2,256,512]{2,1,0:T(8,128)(2,1)} %pad_maximum_fusion.1), channel_id=1, source_target_pairs={{0,6},{2,8},{4,10},{6,12},{8,14},{10,16},{12,18},{14,20},{16,22},{... | collective-permute-start | bytes 1572872 | tf_op jit(solution)/shard_map/ppermute | solution.py:15
  43.1 35.7 %collective-permute-start.5 = (bf16[2,256,512]{2,1,0:T(8,128)(2,1)}, bf16[2,256,512]{2,1,0:T(8,128)(2,1)S(1)}, u32[]{:S(2)}, u32[]{:S(2)}) collective-permute-start(bf16[2,256,512]{2,1,0:T(8,128)(2,1)} %pad_maximum_fusion.1), channel_id=1, source_target_pairs={{6,0},{8,2},{10,4},{12,6},{14,8},{16,10},{18,12},{20,14},{22,16},{... | collective-permute-start | bytes 1572872 | tf_op jit(solution)/shard_map/ppermute | solution.py:15
  49.3 37.7 %collective-permute-start.6 = (bf16[2,256,512]{2,1,0:T(8,128)(2,1)}, bf16[2,256,512]{2,1,0:T(8,128)(2,1)S(1)}, u32[]{:S(2)}, u32[]{:S(2)}) collective-permute-start(bf16[2,256,512]{2,1,0:T(8,128)(2,1)} %pad_maximum_fusion.1), channel_id=1, source_target_pairs={{0,8},{2,10},{4,12},{6,14},{8,16},{10,18},{12,20},{14,22},{16,24},... | collective-permute-start | bytes 1572872 | tf_op jit(solution)/shard_map/ppermute | solution.py:15
  54.2 34.8 %collective-permute-start.7 = (bf16[2,256,512]{2,1,0:T(8,128)(2,1)}, bf16[2,256,512]{2,1,0:T(8,128)(2,1)S(1)}, u32[]{:S(2)}, u32[]{:S(2)}) collective-permute-start(bf16[2,256,512]{2,1,0:T(8,128)(2,1)} %pad_maximum_fusion.1), channel_id=1, source_target_pairs={{8,0},{10,2},{12,4},{14,6},{16,8},{18,10},{20,12},{22,14},{24,16},... | collective-permute-start | bytes 1572872 | tf_op jit(solution)/shard_map/ppermute | solution.py:15
  70.7 26.2 %collective-permute-start.8 = (bf16[2,256,512]{2,1,0:T(8,128)(2,1)}, bf16[2,256,512]{2,1,0:T(8,128)(2,1)S(1)}, u32[]{:S(2)}, u32[]{:S(2)}) collective-permute-start(bf16[2,256,512]{2,1,0:T(8,128)(2,1)} %pad_maximum_fusion.1), channel_id=1, source_target_pairs={{0,10},{2,12},{4,14},{6,16},{8,18},{10,20},{12,22},{14,24},{16,26}... | collective-permute-start | bytes 1572872 | tf_op jit(solution)/shard_map/ppermute | solution.py:15
  76.6 22.4 %collective-permute-start.9 = (bf16[2,256,512]{2,1,0:T(8,128)(2,1)}, bf16[2,256,512]{2,1,0:T(8,128)(2,1)S(1)}, u32[]{:S(2)}, u32[]{:S(2)}) collective-permute-start(bf16[2,256,512]{2,1,0:T(8,128)(2,1)} %pad_maximum_fusion.1), channel_id=1, source_target_pairs={{10,0},{12,2},{14,4},{16,6},{18,8},{20,10},{22,12},{24,14},{26,16}... | collective-permute-start | bytes 1572872 | tf_op jit(solution)/shard_map/ppermute | solution.py:15
  78.8 28.5 %collective-permute-start.10 = (bf16[2,256,512]{2,1,0:T(8,128)(2,1)}, bf16[2,256,512]{2,1,0:T(8,128)(2,1)S(1)}, u32[]{:S(2)}, u32[]{:S(2)}) collective-permute-start(bf16[2,256,512]{2,1,0:T(8,128)(2,1)} %pad_maximum_fusion.1), channel_id=1, source_target_pairs={{0,12},{2,14},{4,16},{6,18},{8,20},{10,22},{12,24},{14,26},{16,28}... | collective-permute-start | bytes 1572872 | tf_op jit(solution)/shard_map/ppermute | solution.py:15
  87.0 31.5 %collective-permute-start.11 = (bf16[2,256,512]{2,1,0:T(8,128)(2,1)}, bf16[2,256,512]{2,1,0:T(8,128)(2,1)S(1)}, u32[]{:S(2)}, u32[]{:S(2)}) collective-permute-start(bf16[2,256,512]{2,1,0:T(8,128)(2,1)} %pad_maximum_fusion.1), channel_id=1, source_target_pairs={{12,0},{14,2},{16,4},{18,6},{20,8},{22,10},{24,12},{26,14},{28,16}... | collective-permute-start | bytes 1572872 | tf_op jit(solution)/shard_map/ppermute | solution.py:15
  89.1 30.2 %collective-permute-start.12 = (bf16[2,256,512]{2,1,0:T(8,128)(2,1)}, bf16[2,256,512]{2,1,0:T(8,128)(2,1)S(1)}, u32[]{:S(2)}, u32[]{:S(2)}) collective-permute-start(bf16[2,256,512]{2,1,0:T(8,128)(2,1)} %pad_maximum_fusion.1), channel_id=1, source_target_pairs={{0,14},{2,16},{4,18},{6,20},{8,22},{10,24},{12,26},{14,28},{16,30}... | collective-permute-start | bytes 1572872 | tf_op jit(solution)/shard_map/ppermute | solution.py:15
  96.9 55.7 %collective-permute-start.13 = (bf16[2,256,512]{2,1,0:T(8,128)(2,1)}, bf16[2,256,512]{2,1,0:T(8,128)(2,1)S(1)}, u32[]{:S(2)}, u32[]{:S(2)}) collective-permute-start(bf16[2,256,512]{2,1,0:T(8,128)(2,1)} %pad_maximum_fusion.1), channel_id=1, source_target_pairs={{14,0},{16,2},{18,4},{20,6},{22,8},{24,10},{26,12},{28,14},{30,16}... | collective-permute-start | bytes 1572872 | tf_op jit(solution)/shard_map/ppermute | solution.py:15
  99.1 54.4 %collective-permute-start.14 = (bf16[2,256,512]{2,1,0:T(8,128)(2,1)}, bf16[2,256,512]{2,1,0:T(8,128)(2,1)S(1)}, u32[]{:S(2)}, u32[]{:S(2)}) collective-permute-start(bf16[2,256,512]{2,1,0:T(8,128)(2,1)} %pad_maximum_fusion.1), channel_id=1, source_target_pairs={{0,16},{2,18},{4,20},{6,22},{8,24},{10,26},{12,28},{14,30},{16,32}... | collective-permute-start | bytes 1572872 | tf_op jit(solution)/shard_map/ppermute | solution.py:15
  107.3 47.0 %collective-permute-start.15 = (bf16[2,256,512]{2,1,0:T(8,128)(2,1)}, bf16[2,256,512]{2,1,0:T(8,128)(2,1)S(1)}, u32[]{:S(2)}, u32[]{:S(2)}) collective-permute-start(bf16[2,256,512]{2,1,0:T(8,128)(2,1)} %pad_maximum_fusion.1), channel_id=1, source_target_pairs={{16,0},{18,2},{20,4},{22,6},{24,8},{26,10},{28,12},{30,14},{32,16}... | collective-permute-start | bytes 1572872 | tf_op jit(solution)/shard_map/ppermute | solution.py:15
where the time goes:
time: 523 us; the launch traced here: 515 us
  local copies, waits for them, and re-layouts  174 us (33%)
  loops' own time  112 us (21%)
  starting transfers between devices  69.4 us (13%)
  blocking collectives  62.8 us (12%)
  waiting for transfers between devices  61.8 us (12%)
  matrix products  25.4 us (5%)
  other arithmetic  8.63 us (2%)
    dynamic_slice x132, local copies, waits for them, and re-layouts, fold_keys(): lax.scan(one_step, carry, (key_stack, value_stack, jnp.arange(count, dtyp...  112 us
    another operation x17, loops' own time, fold_keys(): lax.scan(one_step, carry, (key_stack, value_stack, jnp.arange(count, dtyp...  111 us
    all_to_all x1, blocking collectives, on_device(): lax.all_to_all(attended, 'head', split_axis=0, concat_axis=1, tiled=True)  62.8 us
    ppermute x16, starting transfers between devices, from_behind(): return lax.ppermute(x, axis, pairs)  58.6 us
    ppermute x16, waiting for transfers between devices, from_behind(): return lax.ppermute(x, axis, pairs)  54.8 us
    dynamic_slice x35, local copies, waits for them, and re-layouts, block_place(): lax.dynamic_index_in_dim(block_docs, safe_block, keepdims=False)  21.2 us
    dot_general x8, matrix products, take(): jnp.einsum('hgqk,khd->qhgd', weight.astype(jnp.bfloat16), value_three, pr...  17.6 us
    slice x16, local copies, waits for them, and re-layouts, fold_keys(): value_stack = piece[1].reshape(count, MASK_BLOCK_SIZE, piece.shape[2])  15.6 us
  transfers between devices with their start and end apart: 19, of which 5 were waited for; matrix products, arithmetic and copies ran while one was open for 4% of the time, Pallas kernels for 0%

commit v1 on v0

v1 whole, which is shorter than its diff:
```python
import functools
import math

import jax
import jax.numpy as jnp
from jax import lax
from jax.experimental import pallas as pl
from jax.experimental.pallas import tpu as pltpu
from jax.sharding import PartitionSpec as P

D = 128
T = 128
MESH = pl.DeviceIdType.MESH

HOPS = (
    ((1, 0, 0, 1, 3, 1), (1, 0, 0, 3, 1, -1), (1, 1, 0, 2, 3, 1), (1, 2, 0, 3, 3, 1),
     (1, 1, 0, 1, 4, 0), (1, 2, 0, 2, 4, 0), (1, 3, 0, 3, 4, 0), (2, 3, 1, 2, 2, -1),
     (2, 2, 3, 3, 2, 1), (2, 1, 3, 1, 7, 0), (2, 3, 1, 3, 5, 0), (2, 1, 4, 0, 5, -1),
     (2, 1, 4, 2, 7, 1), (2, 2, 4, 1, 5, -1), (2, 3, 3, 3, 7, 0), (2, 3, 4, 0, 7, 1),
     (2, 3, 4, 2, 5, -1), (3, 0, 5, 0, 1, 0), (3, 1, 5, 1, 1, 0), (3, 0, 7, 0, 3, 0),
     (3, 2, 5, 2, 1, 0), (3, 1, 7, 0, 4, -1), (3, 1, 7, 2, 6, 1), (3, 0, 5, 3, 6, -1),
     (3, 3, 7, 0, 6, 1), (3, 0, 7, 1, 6, 1), (4, 1, 1, 0, 2, -1), (4, 2, 1, 1, 2, -1)),
    ((1, 0, 0, 1, 3, 1), (1, 0, 0, 3, 1, -1), (1, 1, 0, 2, 3, 1), (1, 2, 0, 3, 3, 1),
     (1, 0, 0, 0, 4, 0), (1, 1, 0, 1, 4, 0), (1, 2, 0, 2, 4, 0), (1, 3, 0, 3, 4, 0),
     (2, 3, 1, 2, 2, -1), (2, 2, 3, 3, 2, 1), (2, 0, 4, 1, 7, 1), (2, 0, 4, 3, 5, -1),
     (2, 1, 4, 0, 5, -1), (2, 1, 4, 2, 7, 1), (2, 2, 4, 1, 5, -1), (2, 3, 3, 3, 7, 0),
     (2, 3, 4, 0, 7, 1), (2, 3, 4, 2, 5, -1), (3, 0, 5, 0, 1, 0), (3, 1, 5, 1, 1, 0),
     (3, 0, 7, 0, 3, 0), (3, 2, 5, 2, 1, 0), (3, 2, 2, 2, 6, 0), (3, 2, 7, 3, 6, 1),
     (3, 3, 7, 0, 6, 1), (3, 0, 7, 1, 6, 1), (4, 1, 1, 0, 2, -1), (4, 2, 1, 1, 2, -1)),
)
DEPTH = 4
MAX_OUT = 9


def tables():
    arrive = [[[] for _ in range(4)] for _ in HOPS]
    send = [[{} for _ in range(4)] for _ in HOPS]
    for u, hops in enumerate(HOPS):
        count = [0] * 4
        for depth, src, s_slot, dst, d_slot, move in hops:
            arrive[u][dst].append((depth, d_slot))
            send[u][src].setdefault(s_slot, []).append((d_slot, move, count[src]))
            count[src] += 1
    return arrive, send


ARRIVE, SEND = tables()


def kernel(heads, group, blk_count,
           docs, q_hbm, k_hbm, v_hbm, o_hbm,
           window, q_all, o_all, bias,
           own_sem, q_sem, o_sem, send_sem, recv_sem):
    blk, half = lax.axis_index("blk"), lax.axis_index("head")
    blocks = 2 * blk_count
    rows = blocks // 4
    me = jnp.where(half == 0, blk, blocks - 1 - blk)
    r, j = me // 4, lax.rem(me, 4)

    def device(row, col):
        at = 4 * lax.rem(row + rows, rows) + lax.rem(col + 4, 4)
        early = at < blk_count
        return {"blk": jnp.where(early, at, blocks - 1 - at), "head": jnp.where(early, 0, 1)}

    to = {0: device(r + 1, j), 1: device(r, j + 1), -1: device(r, j - 1)}

    def own_copy(u, h):
        cols = pl.ds(pl.multiple_of(h * D, D), D)
        return pltpu.make_async_copy(
            (k_hbm, v_hbm)[u].at[:, cols], window.at[u, h, 0], own_sem.at[u, h])

    def q_copy(n, h):
        cols = pl.ds(pl.multiple_of(n * D, D), D)
        return pltpu.make_async_copy(q_hbm.at[:, cols], q_all.at[n], q_sem.at[h])

    def o_copy(n, h):
        cols = pl.ds(pl.multiple_of(n * D, D), D)
        return pltpu.make_async_copy(o_all.at[n], o_hbm.at[:, cols], o_sem.at[h])

    def hop(u, h, s_slot, d_slot, move, number):
        return pltpu.make_async_remote_copy(
            src_ref=window.at[u, h, s_slot], dst_ref=window.at[u, h, d_slot],
            send_sem=send_sem.at[u, h, number], recv_sem=recv_sem.at[u, h, d_slot],
            device_id=to[move], device_id_type=MESH)

    @pl.loop(0, heads)
    def _(h):
        for u in range(2):
            own_copy(u, h).start()

    barrier = pltpu.get_barrier_semaphore()
    for there in (to[0], to[1], to[-1], device(r - 1, j)):
        pl.semaphore_signal(barrier, inc=1, device_id=there, device_id_type=MESH)

    my_doc = docs[me]
    for slot in range(8):
        col = lax.rem(j + slot, 4)
        if slot < 4:
            at = 4 * r + col - jnp.where(col > j, 8, 0)
        else:
            at = 4 * r - 4 + col
        same = (at >= 0) & (docs[jnp.maximum(at, 0)] == my_doc)
        bias[:, slot * T:(slot + 1) * T] = jnp.full(
            (8, T), jnp.where(same, 0.0, -jnp.inf), jnp.float32)

    pl.semaphore_wait(barrier, 4)

    scale = 1.0 / math.sqrt(D)

    def attend(h, part, parts):
        count = group // parts
        first = h * group + part * count
        key = window[0, h].reshape(8 * T, D)
        value = window[1, h].reshape(8 * T, D)
        row = lax.broadcasted_iota(jnp.int32, (1, T, T), 1)
        column = lax.broadcasted_iota(jnp.int32, (1, T, T), 2)
        causal = jnp.broadcast_to(column <= row, (count, T, T)).reshape(count * T, T)
        query = q_all[pl.ds(first, count)].reshape(count * T, D)
        score = lax.dot_general(query, key, (((1,), (1,)), ((), ())),
                                preferred_element_type=jnp.float32)
        own = jnp.where(causal, score[:, :T], -jnp.inf)
        rest = score[:, T:] + bias[0:1, T:]
        top = jnp.maximum(jnp.max(own, axis=1, keepdims=True),
                          jnp.max(rest, axis=1, keepdims=True))
        weight = jnp.concatenate(
            [jnp.exp((own - top) * scale), jnp.exp((rest - top) * scale)], axis=1)
        total = jnp.sum(weight, axis=1, keepdims=True)
        summed = jnp.dot(weight.astype(jnp.bfloat16), value, preferred_element_type=jnp.float32)
        out = (summed / total).astype(jnp.bfloat16)
        o_all[pl.ds(first, count)] = out.reshape(count, T, D)

    @pl.loop(0, heads + DEPTH + 1)
    def _(i):
        @pl.when(i < heads)
        def _():
            @pl.loop(0, group)
            def _(g):
                q_copy(i * group + g, i).start()
            for u in range(2):
                own_copy(u, i).wait()

        done = i - DEPTH - 1
        for u in range(2):
            for col in range(4):
                @pl.when(j == col)
                def _(u=u, col=col):
                    for depth in range(DEPTH, -1, -1):
                        h = i - depth
                        slots = ([0] if depth == 0 else
                                 [s for d, s in ARRIVE[u][col] if d == depth])
                        if not slots:
                            continue

                        @pl.when((h >= 0) & (h < heads))
                        def _(h=h, slots=slots, depth=depth):
                            for slot in slots:
                                if depth:
                                    hop(u, h, slot, slot, 1, 0).wait_recv()
                                for d_slot, move, number in SEND[u][col].get(slot, ()):
                                    hop(u, h, slot, d_slot, move, number).start()

            @pl.when(done >= 0)
            def _(u=u):
                if u == 0:
                    pltpu.make_async_copy(
                        o_all.at[pl.ds(done * group, group)],
                        q_all.at[pl.ds(done * group, group)], q_sem.at[done]).wait()
                attend(done, u, 2)

                @pl.loop(0, group // 2)
                def _(g):
                    o_copy(done * group + u * (group // 2) + g, done).start()

    @pl.loop(0, heads)
    def _(h):
        pltpu.make_async_copy(
            q_all.at[pl.ds(h * group, group)],
            o_all.at[pl.ds(h * group, group)], o_sem.at[h]).wait()
        for u in range(2):
            for col in range(4):
                @pl.when(j == col)
                def _(u=u, col=col):
                    for slot, outs in SEND[u][col].items():
                        for d_slot, move, number in outs:
                            hop(u, h, slot, d_slot, move, number).wait_send()


def on_device(queries, keys, values, block_docs):
    blk_count = lax.axis_size("blk")
    heads = keys.shape[1] // D
    group = queries.shape[1] // keys.shape[1]
    anywhere = pl.BlockSpec(memory_space=pl.ANY)
    return pl.pallas_call(
        functools.partial(kernel, heads, group, blk_count),
        out_shape=jax.ShapeDtypeStruct(queries.shape, jnp.bfloat16),
        in_specs=[pl.BlockSpec(memory_space=pltpu.SMEM), anywhere, anywhere, anywhere],
        out_specs=anywhere,
        scratch_shapes=[
            pltpu.VMEM((2, heads, 8, T, D), jnp.bfloat16),
            pltpu.VMEM((heads * group, T, D), jnp.bfloat16),
            pltpu.VMEM((heads * group, T, D), jnp.bfloat16),
            pltpu.VMEM((8, 8 * T), jnp.float32),
            pltpu.SemaphoreType.DMA((2, heads)),
            pltpu.SemaphoreType.DMA((heads,)),
            pltpu.SemaphoreType.DMA((heads,)),
            pltpu.SemaphoreType.DMA((2, heads, MAX_OUT)),
            pltpu.SemaphoreType.DMA((2, heads, 8)),
        ],
        compiler_params=pltpu.CompilerParams(
            collective_id=0, has_side_effects=True, vmem_limit_bytes=48 << 20),
        name="window_attention",
    )(block_docs, queries, keys, values)


def solution(mesh):
    rows = P(("dp", "blk", "head"), None)
    return jax.shard_map(
        on_device, mesh=mesh, in_specs=(rows, rows, rows, P("dp")), out_specs=rows,
        check_vma=False)
```

time: 523 us -> 82.3 us (0.16)
  the two profiles are of different devices: /device:TPU:3 before, /device:TPU:0 now
where the time goes in v1:
time: 82.3 us; the launch traced here: 82.1 us
  Pallas kernels  76.6 us (93%)
  local copies, waits for them, and re-layouts  5.47 us (7%)
    pallas_call x1, Pallas kernels, on_device(): pl.pallas_call(functools.partial(kernel, heads, group, blk_count), out_sh...  76.6 us
    unnamed x9, local copies, waits for them, and re-layouts  5.47 us

profile of v1, /device:TPU:0, one launch (start us, length us, event | category | flops | bytes accessed | tf_op | source)
XLA Modules:
  0.0 82.1 jit_solution(10080218423462210297)
XLA Ops:
  0.0 0.0 copy-start
  0.0 1.6 %copy-done = bf16[128,8192]{1,0:T(8,128)(2,1)S(1)} copy-done((bf16[128,8192]{1,0:T(8,128)(2,1)S(1)}, bf16[128,8192]{1,0:T(8,128)(2,1)}, u32[]{:S(2)}) %copy-start) | copy-done | bytes 2097176
  1.6 0.0 copy-start.1
  1.6 0.9 %copy-done.1 = bf16[128,1024]{1,0:T(8,128)(2,1)S(1)} copy-done((bf16[128,1024]{1,0:T(8,128)(2,1)S(1)}, bf16[128,1024]{1,0:T(8,128)(2,1)}, u32[]{:S(2)}) %copy-start.1) | copy-done | bytes 262168
  2.5 0.0 copy-start.2
  2.5 0.9 %copy-done.2 = bf16[128,1024]{1,0:T(8,128)(2,1)S(1)} copy-done((bf16[128,1024]{1,0:T(8,128)(2,1)S(1)}, bf16[128,1024]{1,0:T(8,128)(2,1)}, u32[]{:S(2)}) %copy-start.2) | copy-done | bytes 262168
  3.5 0.0 copy-start.3
  3.5 0.7 copy-done.3
  4.1 76.6 %window_attention.1 = bf16[128,8192]{1,0:T(8,128)(2,1)S(1)} custom-call(s32[64]{0:T(128)S(1)} %copy-done.3, bf16[128,8192]{1,0:T(8,128)(2,1)S(1)} %copy-done, bf16[128,1024]{1,0:T(8,128)(2,1)S(1)} %copy-done.1, bf16[128,1024]{1,0:T(8,128)(2,1)S(1)} %copy-done.2), custom_call_target="tpu_custom_call" | custom-call | tf_op jit(solution)/shard_map/window_attention/pallas_call | solution.py:193
  80.7 1.3 %copy.6 = bf16[128,8192]{1,0:T(8,128)(2,1)} copy(bf16[128,8192]{1,0:T(8,128)(2,1)S(1)} %window_attention.1) | data formatting | bytes 4194304
Async XLA Ops:
  0.0 1.6 %copy-start = (bf16[128,8192]{1,0:T(8,128)(2,1)S(1)}, bf16[128,8192]{1,0:T(8,128)(2,1)}, u32[]{:S(2)}) copy-start(bf16[128,8192]{1,0:T(8,128)(2,1)} %q_hbm.1) | copy-start | bytes 6291460
  1.6 0.9 %copy-start.1 = (bf16[128,1024]{1,0:T(8,128)(2,1)S(1)}, bf16[128,1024]{1,0:T(8,128)(2,1)}, u32[]{:S(2)}) copy-start(bf16[128,1024]{1,0:T(8,128)(2,1)} %k_hbm.1) | copy-start | bytes 786436
  2.5 0.9 %copy-start.2 = (bf16[128,1024]{1,0:T(8,128)(2,1)S(1)}, bf16[128,1024]{1,0:T(8,128)(2,1)}, u32[]{:S(2)}) copy-start(bf16[128,1024]{1,0:T(8,128)(2,1)} %v_hbm.1) | copy-start | bytes 786436
  3.5 0.7 copy-start.3

commit v2 on v1

v2 whole, which is shorter than its diff:
```python
import functools
import math

import jax
import jax.numpy as jnp
from jax import lax
from jax.experimental import pallas as pl
from jax.experimental.pallas import tpu as pltpu
from jax.sharding import PartitionSpec as P

D = 128
T = 128
BLOCKS = 64
SPAN = 8
MESH = pl.DeviceIdType.MESH

TREES = (
    (1, 3, 194, 4, 69, 263, 454,),
    (64, 66, 131, 69, 324, 134, 199, 12, 776,),
    (131, 134, 389, 324, 263, 329, 584,),
    (199, 452, 454, 389, 264, 394, 649,),
    (261, 326, 264, 521, 523, 711, 425, 2661, 2378,),
    (326, 391, 329, 584, 586, 459, 524,),
    (386, 129, 391, 394, 649, 77, 844, 488, 2596, 2315, 712,),
    (451, 192, 459, 712, 714, 12, 781, 841, 693, 3441, 3150,),
    (521, 523, 714, 524, 589, 846, 756, 3376, 3087,),
    (586, 651, 589, 844, 654, 783, 819, 3327, 4048,),
    (651, 654, 909, 719, 972, 882, 3262, 3985, 1104,),
    (719, 972, 974, 909, 929, 2157, 2898, 819, 3292, 1808, 1041,),
    (781, 783, 974, 803, 2287, 3024, 1041, 1106, 1043,),
    (846, 911, 866, 2222, 2961, 1104, 1106, 1171, 1044,),
    (898, 911, 992, 2092, 2835, 1232, 189, 3922, 1169, 1109, 1364,),
    (1008, 3103, 2003, 1232, 1234, 1169, 1044, 1301, 1174,),
    (1043, 1234, 1239, 1492, 1494, 1429, 1361,),
    (1109, 1364, 1366, 1426, 1303, 1491, 1304,),
    (1171, 1174, 1429, 1369, 1624, 1556, 1276, 3896, 3607,),
    (1239, 1492, 1494, 1434, 1689, 1621, 1323, 2791, 2520,),
    (1301, 1303, 1304, 1561, 1499, 1754, 1686,),
    (1366, 1431, 1369, 1624, 1626, 1563, 1564,),
    (1431, 1434, 1689, 1629, 1884, 1816, 1823, 2011,),
    (1499, 1752, 1754, 1564, 1694, 1949, 1881,),
    (1561, 1563, 1759, 2014, 1946, 1591, 3571, 3292, 1821,),
    (1626, 1691, 1629, 1884, 1886, 1823, 2016,),
    (1691, 1694, 1949, 1951, 2012, 1953, 2144,),
    (1759, 2012, 1821, 2014, 2016, 2081, 1890,),
    (1827, 2272, 2079, 2274, 2205, 2209, 2142,),
    (1890, 2209, 2142, 2211, 2272, 2079, 2084,),
    (1946, 1951, 1953, 2144, 2146, 2083, 1701, 2404,),
    (2011, 1764, 2336, 2083, 2341, 2401, 2406, 2466,),
    (2081, 2084, 2149, 2343, 2531, 2274, 2534,),
    (2146, 2211, 2149, 2404, 2331, 1751, 2214, 2279, 1512,),
    (2214, 2469, 2471, 2531, 2532, 2409, 2664,),
    (2279, 2532, 2534, 2469, 2344, 2474, 2729,),
    (2341, 2406, 2343, 2504, 516, 2344, 2601, 299, 2794,),
    (2409, 2664, 2666, 2726, 2603, 2791, 2604,),
    (2471, 2474, 2729, 2539, 2792, 2567, 451, 236, 2669,),
    (2539, 2792, 2601, 2794, 2604, 2734, 2989,),
    (2583, 1491, 2603, 2772, 1296, 1260, 2861, 2921, 1071, 3054, 2986,),
    (2666, 2693, 321, 2731, 2669, 2924, 2848, 2063, 110, 2863, 1008,),
    (2731, 2734, 2989, 2913, 2126, 2799, 3052, 945, 3184,),
    (2799, 3052, 2819, 194, 173, 3054, 2978, 2205, 1886, 1969, 1906, 252, 3888,),
    (2835, 1247, 2861, 2926, 2863, 2032, 3121, 3123, 3314,),
    (2882, 142, 2926, 2991, 3008, 945, 3184, 3186, 3124, 63, 4083,),
    (2945, 2991, 126, 4018, 3249, 3251, 3312, 3189, 3444,),
    (3043, 2268, 1843, 3312, 3314, 3249, 3124, 3381, 3254,),
    (3121, 3123, 3189, 3444, 3446, 3506, 3319,),
    (3186, 3251, 3197, 3961, 3701, 3446, 3704, 3636, 3383,),
    (3254, 3509, 3511, 3571, 3572, 3339, 711, 504, 3449,),
    (3319, 3572, 3574, 3509, 3384, 3514, 3769,),
    (3381, 3418, 1686, 3383, 3574, 3384, 1465, 3643, 3834,),
    (3449, 3704, 3706, 3766, 3643, 3831, 3644,),
    (3511, 3514, 3769, 3579, 3832, 3709, 3964,),
    (3579, 3832, 3641, 3834, 3644, 3709, 3774,),
    (3636, 3376, 3641, 3132, 3901, 3903, 4091, 4094, 4026,),
    (3670, 1426, 3706, 3733, 1361, 3771, 3796, 1296, 1213, 3964, 1150, 1087,),
    (3771, 3774, 4029, 3839, 4092,),
    (3839, 4092, 4094, 4029,),
    (3901, 3966, 3903,),
    (3966, 4031,),
    (4031,),
)


def programs():
    arrive = [{} for _ in range(BLOCKS)]
    send = [{} for _ in range(BLOCKS)]
    extra = [SPAN] * BLOCKS
    count = [0] * BLOCKS
    for block, hops in enumerate(TREES):
        slot, depth = {block: 0}, {block: 0}
        for hop in hops:
            src, dst = hop // BLOCKS, hop % BLOCKS
            depth[dst] = depth[src] + 1
            if 0 < dst - block < SPAN:
                slot[dst] = dst - block
            else:
                slot[dst] = extra[dst]
                extra[dst] += 1
            arrive[dst].setdefault(depth[dst], []).append(slot[dst])
            send[src].setdefault(slot[src], []).append((dst, slot[dst], count[src]))
            count[src] += 1
    deepest = max(max(a) for a in arrive if a)
    return arrive, send, max(extra), max(count), deepest


ARRIVE, SEND, SLOTS, MAX_OUT, DEPTH = programs()
PARTS = 4
OFFSET = tuple(2 * d for d in range(DEPTH + 1))


def kernel(heads, group, blk_count,
           docs, q_hbm, k_hbm, v_hbm, o_hbm,
           window, q_all, o_all, bias,
           own_sem, q_sem, o_sem, send_sem, recv_sem):
    blk, half = lax.axis_index("blk"), lax.axis_index("head")
    me = jnp.where(half == 0, blk, BLOCKS - 1 - blk)
    z_hi, x, y = blk // 16, lax.rem(blk // 4, 4), lax.rem(blk, 4)

    def own_copy(u, h):
        cols = pl.ds(pl.multiple_of(h * D, D), D)
        return pltpu.make_async_copy(
            (k_hbm, v_hbm)[u].at[:, cols], window.at[h, 0, u], own_sem.at[u, h])

    def q_copy(n, h):
        cols = pl.ds(pl.multiple_of(n * D, D), D)
        return pltpu.make_async_copy(q_hbm.at[:, cols], q_all.at[n], q_sem.at[h])

    def o_copy(n, h):
        cols = pl.ds(pl.multiple_of(n * D, D), D)
        return pltpu.make_async_copy(o_all.at[n], o_hbm.at[:, cols], o_sem.at[h])

    def hop(h, s_slot, d_slot, there, number):
        early = there < BLOCKS // 2
        return pltpu.make_async_remote_copy(
            src_ref=window.at[h, s_slot], dst_ref=window.at[h, d_slot],
            send_sem=send_sem.at[h, number], recv_sem=recv_sem.at[h, d_slot],
            device_id={"blk": there if early else BLOCKS - 1 - there, "head": 0 if early else 1},
            device_id_type=MESH)

    def on_block(body, low=0, high=BLOCKS):
        if high - low == 1:
            return body(low)
        mid = (low + high) // 2

        @pl.when(me < mid)
        def _():
            on_block(body, low, mid)

        @pl.when(me >= mid)
        def _():
            on_block(body, mid, high)

    @pl.loop(0, heads)
    def _(h):
        for u in range(2):
            own_copy(u, h).start()

    barrier = pltpu.get_barrier_semaphore()
    for dx, dy, dz in ((1, 0, 0), (3, 0, 0), (0, 1, 0), (0, 3, 0), (0, 0, 1), (0, 0, 3)):
        z = lax.rem(2 * z_hi + half + dz, 4)
        there = {"blk": z // 2 * 16 + lax.rem(x + dx, 4) * 4 + lax.rem(y + dy, 4),
                 "head": lax.rem(z, 2)}
        pl.semaphore_signal(barrier, inc=1, device_id=there, device_id_type=MESH)

    my_doc = docs[me]
    for slot in range(SPAN):
        at = me - slot
        same = (at >= 0) & (docs[jnp.maximum(at, 0)] == my_doc)
        bias[slot * T:(slot + 1) * T] = jnp.where(
            lax.broadcasted_iota(jnp.int32, (T, D), 1) == 0,
            jnp.where(same, 0.0, -1e30), 0.0).astype(jnp.bfloat16)

        @pl.when(at < 0)
        def _(slot=slot):
            @pl.loop(0, heads)
            def _(h):
                window[h, slot] = jnp.zeros((2, T, D), jnp.bfloat16)

    pl.semaphore_wait(barrier, 6)

    lane = lax.broadcasted_iota(jnp.int32, (1, D), 1)
    factor = math.log2(math.e) / math.sqrt(D)

    def attend(h, part, parts):
        count = group // parts
        first = h * group + part * count
        key = jnp.concatenate([window[h, :SPAN, 0].reshape(SPAN * T, D), bias[...]], axis=1)
        value = jnp.concatenate(
            [window[h, :SPAN, 1].reshape(SPAN * T, D),
             jnp.ones((SPAN * T, D), jnp.bfloat16)], axis=1)
        marker = jnp.broadcast_to(jnp.where(lane == 0, 1.0, 0.0), (count * T, D))
        query = jnp.concatenate(
            [q_all[pl.ds(first, count)].reshape(count * T, D), marker.astype(jnp.bfloat16)], axis=1)
        row = lax.broadcasted_iota(jnp.int32, (1, T, T), 1)
        column = lax.broadcasted_iota(jnp.int32, (1, T, T), 2)
        causal = jnp.broadcast_to(column <= row, (count, T, T)).reshape(count * T, T)
        score = lax.dot_general(query, key, (((1,), (1,)), ((), ())),
                                preferred_element_type=jnp.float32)
        pieces = [jnp.where(causal, score[:, :T], -1e30)]
        pieces += [score[:, n * T:(n + 1) * T] for n in range(1, SPAN)]
        top = jnp.max(functools.reduce(jnp.maximum, pieces), axis=1, keepdims=True)
        weight = jnp.concatenate(
            [jnp.exp2((piece - top) * factor).astype(jnp.bfloat16) for piece in pieces], axis=1)
        summed = jnp.dot(weight, value, preferred_element_type=jnp.float32)
        out = (summed[:, :D] / summed[:, D:]).astype(jnp.bfloat16)
        o_all[pl.ds(first, count)] = out.reshape(count, T, D)

    @pl.loop(0, heads + OFFSET[DEPTH])
    def _(i):
        @pl.when(i < heads)
        def _():
            @pl.loop(0, group)
            def _(g):
                q_copy(i * group + g, i).start()
            for u in range(2):
                own_copy(u, i).wait()

        def travel(block):
            for depth in range(DEPTH, -1, -1):
                h = i - OFFSET[depth]
                slots = ARRIVE[block].get(depth, []) if depth else [0]
                if not slots:
                    continue

                @pl.when((h >= 0) & (h < heads))
                def _(h=h, slots=slots, depth=depth):
                    for slot in slots:
                        if depth:
                            hop(h, slot, slot, (block + 1) % BLOCKS, 0).wait_recv()
                        for there, d_slot, number in SEND[block].get(slot, ()):
                            hop(h, slot, d_slot, there, number).start()

        on_block(travel)
        done = i - OFFSET[DEPTH]

        @pl.when(done >= 0)
        def _():
            pltpu.make_async_copy(
                o_all.at[pl.ds(done * group, group)],
                q_all.at[pl.ds(done * group, group)], q_sem.at[done]).wait()
            for part in range(PARTS):
                attend(done, part, PARTS)

            @pl.loop(0, group)
            def _(g):
                o_copy(done * group + g, done).start()

    def finish(block):
        @pl.loop(0, heads)
        def _(h):
            for slot, outs in SEND[block].items():
                for there, d_slot, number in outs:
                    hop(h, slot, d_slot, there, number).wait_send()

    on_block(finish)

    @pl.loop(0, heads)
    def _(h):
        pltpu.make_async_copy(
            q_all.at[pl.ds(h * group, group)],
            o_all.at[pl.ds(h * group, group)], o_sem.at[h]).wait()


def on_device(queries, keys, values, block_docs):
    blk_count = lax.axis_size("blk")
    heads = keys.shape[1] // D
    group = queries.shape[1] // keys.shape[1]
    anywhere = pl.BlockSpec(memory_space=pltpu.HBM)
    return pl.pallas_call(
        functools.partial(kernel, heads, group, blk_count),
        out_shape=jax.ShapeDtypeStruct(queries.shape, jnp.bfloat16),
        in_specs=[pl.BlockSpec(memory_space=pltpu.SMEM), anywhere, anywhere, anywhere],
        out_specs=anywhere,
        scratch_shapes=[
            pltpu.VMEM((heads, SLOTS, 2, T, D), jnp.bfloat16),
            pltpu.VMEM((heads * group, T, D), jnp.bfloat16),
            pltpu.VMEM((heads * group, T, D), jnp.bfloat16),
            pltpu.VMEM((SPAN * T, D), jnp.bfloat16),
            pltpu.SemaphoreType.DMA((2, heads)),
            pltpu.SemaphoreType.DMA((heads,)),
            pltpu.SemaphoreType.DMA((heads,)),
            pltpu.SemaphoreType.DMA((heads, MAX_OUT)),
            pltpu.SemaphoreType.DMA((heads, SLOTS)),
        ],
        compiler_params=pltpu.CompilerParams(
            collective_id=0, has_side_effects=True, vmem_limit_bytes=62 << 20),
        name="window_attention",
    )(block_docs, queries, keys, values)


def solution(mesh):
    rows = P(("dp", "blk", "head"), None)
    return jax.shard_map(
        on_device, mesh=mesh, in_specs=(rows, rows, rows, P("dp")), out_specs=rows,
        check_vma=False)
```

time: 82.3 us -> 57.2 us (0.70)
  Pallas kernels: 76.6 us -> 53.9 us
  local copies, waits for them, and re-layouts: 5.47 us -> 3.1 us
    pallas_call x1, Pallas kernels: 76.6 us -> 53.9 us  [on_device(): pl.pallas_call(functools.partial(kernel, heads, group, blk_count), out_sh...]
    unnamed x9 -> x1, local copies, waits for them, and re-layouts: 5.47 us -> 3.1 us
where the time goes in v2:
time: 57.2 us; the launch traced here: 57 us
  Pallas kernels  53.9 us (94%)
  local copies, waits for them, and re-layouts  3.1 us (5%)
    pallas_call x1, Pallas kernels, on_device(): pl.pallas_call(functools.partial(kernel, heads, group, blk_count), out_sh...  53.9 us
    unnamed x1, local copies, waits for them, and re-layouts  3.1 us

profile of v2, /device:TPU:0, one launch (start us, length us, event | category | flops | bytes accessed | tf_op | source)
XLA Modules:
  0.0 57.0 jit_solution(10463608795588959266)
XLA Ops:
  0.0 53.9 %window_attention.1 = bf16[128,8192]{1,0:T(8,128)(2,1)} custom-call(s32[64]{0:T(128)} %docs.1, bf16[128,8192]{1,0:T(8,128)(2,1)} %q_hbm.1, bf16[128,1024]{1,0:T(8,128)(2,1)} %k_hbm.1, bf16[128,1024]{1,0:T(8,128)(2,1)} %v_hbm.1), custom_call_target="tpu_custom_call" | custom-call | tf_op jit(solution)/shard_map/window_attention/pallas_call | solution.py:269
  53.9 3.1 %copy.6 = bf16[128,8192]{1,0:T(8,128)(2,1)} copy(bf16[128,8192]{1,0:T(8,128)(2,1)} %window_attention.1) | data formatting | bytes 4194304

commit v3 on v2

v3 whole, which is shorter than its diff:
```python
import functools
import math

import jax
import jax.numpy as jnp
from jax import lax
from jax.experimental import pallas as pl
from jax.experimental.pallas import tpu as pltpu
from jax.sharding import PartitionSpec as P

D = 128
T = 128
BLOCKS = 64
SPAN = 8
MESH = pl.DeviceIdType.MESH

TREES = (
    (1, 3, 194, 4, 69, 263, 454,),
    (66, 131, 69, 324, 134, 299, 2791, 2504, 236, 2856, 2567,),
    (131, 134, 389, 324, 199, 329, 584,),
    (199, 452, 261, 454, 264, 394, 649,),
    (261, 326, 263, 264, 521, 523, 714,),
    (321, 64, 326, 391, 329, 586, 459, 712, 12,),
    (391, 394, 649, 584, 651, 589, 844,),
    (459, 712, 521, 714, 524, 654, 909,),
    (523, 524, 781, 841, 719, 974, 906,),
    (586, 589, 844, 768, 783, 971, 16, 693, 3441, 3150,),
    (651, 711, 451, 192, 12, 654, 909, 833, 207, 16, 81,),
    (719, 972, 974, 898, 129, 77, 81, 146, 803, 2268, 1808,),
    (781, 846, 783, 796, 1808, 1041, 1106, 992, 2092, 2835,),
    (846, 911, 861, 1873, 1104, 1106, 1043, 1044,),
    (911, 963, 211, 1232, 926, 1938, 1169, 1949, 1881, 1621, 1364,),
    (991, 2003, 1232, 1234, 1169, 1044, 1301, 1174,),
    (1041, 1043, 1234, 1109, 1239, 1492, 1494,),
    (1104, 1109, 1366, 1426, 1171, 1052, 1816, 1556, 1303,),
    (1171, 1174, 1429, 1364, 1431, 1304, 1561,),
    (1239, 1492, 1494, 1429, 1304, 1369, 1434,),
    (1301, 1303, 1499, 1752, 1754, 1686, 1386, 2726, 2457,),
    (1366, 1369, 1624, 1563, 1751, 1564, 1449, 2661, 2394,),
    (1431, 1491, 1434, 1689, 1624, 1247, 2012, 1821, 1528, 3636, 3355,),
    (1499, 1752, 1754, 1689, 1564, 1629, 1694,),
    (1561, 1626, 1563, 1759, 2014, 1654, 3506, 3229, 1591, 3571, 3292,),
    (1626, 1691, 1629, 1884, 1886, 1823, 1827, 2272,),
    (1691, 1694, 1949, 1884, 1759, 2016, 1701, 2401,),
    (1764, 2336, 2079, 2012, 2081, 2142, 2146, 2205,),
    (1821, 1823, 2014, 1953, 1890, 1827, 2272,),
    (1886, 1951, 1890, 2209, 2144, 2211, 2084,),
    (1946, 1951, 1953, 2144, 2146, 2083, 1701, 2404,),
    (2011, 2016, 2083, 2274, 2209, 1764, 2341, 2214,),
    (2081, 2084, 2149, 2343, 2531, 2274, 2534,),
    (2149, 2404, 2331, 1751, 2406, 2466, 2343, 2531, 1512,),
    (2211, 2214, 2469, 2378, 646, 2279, 2532, 2344, 425,),
    (2279, 2532, 2534, 2469, 2474, 2729, 2664,),
    (2341, 2344, 2409, 2666, 2726, 2603, 2791,),
    (2406, 2471, 2409, 2664, 2603, 2794, 2604,),
    (2471, 2474, 2729, 2539, 2792, 2669, 2924,),
    (2539, 2792, 2583, 1491, 2601, 2794, 1260, 2734, 2989,),
    (2601, 2630, 386, 389, 321, 362, 2604, 173, 110, 2863, 3051,),
    (2666, 2731, 2772, 1296, 2669, 2924, 2848, 2063, 2926, 1071, 1008,),
    (2731, 2734, 2989, 2799, 3052, 2941, 3953, 3184,),
    (2799, 3052, 2861, 3054, 2876, 3888, 3006, 4018, 3249,),
    (2848, 2861, 2863, 3054, 2096, 3121, 3123, 3314,),
    (2913, 2926, 2991, 3043, 2161, 3184, 3186, 2291, 3124,),
    (2978, 2991, 2226, 3249, 3251, 3312, 3189, 3444,),
    (3071, 4083, 3312, 3121, 3314, 3124, 3381, 3254,),
    (3087, 971, 3123, 756, 3319, 3574, 3506, 3509, 3441,),
    (3186, 3189, 3444, 3339, 711, 3446, 3383, 3571, 504,),
    (3251, 3254, 3509, 3418, 1686, 3319, 3572, 3384, 1465,),
    (3327, 4091, 3831, 3572, 3574, 3832, 3641, 3701, 3514,),
    (3381, 3383, 3384, 3449, 3643, 3834, 3766,),
    (3446, 3465, 581, 3511, 3449, 3704, 3636, 3376, 378, 3579, 3132,),
    (3511, 3528, 516, 3514, 3769, 3704, 315, 3644, 3709,),
    (3579, 3832, 3834, 3769, 3644, 3901, 3774,),
    (3641, 3706, 3643, 3709, 3964, 3774, 3839,),
    (3670, 1426, 3706, 3771, 1213, 3964, 3966, 3903,),
    (3733, 1361, 3771, 3796, 1296, 1150, 4029, 1087, 4092,),
    (3839, 4092, 4094, 4029,),
    (3901, 3903, 4094,),
    (3966, 4031,),
    (4031,),
)


def programs():
    arrive = [{} for _ in range(BLOCKS)]
    send = [{} for _ in range(BLOCKS)]
    extra = [SPAN] * BLOCKS
    count = [0] * BLOCKS
    for block, hops in enumerate(TREES):
        slot, depth = {block: 0}, {block: 0}
        for hop in hops:
            src, dst = hop // BLOCKS, hop % BLOCKS
            depth[dst] = depth[src] + 1
            if 0 < dst - block < SPAN:
                slot[dst] = dst - block
            else:
                slot[dst] = extra[dst]
                extra[dst] += 1
            arrive[dst].setdefault(depth[dst], []).append(slot[dst])
            send[src].setdefault(slot[src], []).append((dst, slot[dst], depth[dst]))
            count[src] += 1
    deepest = max(max(a) for a in arrive if a)
    return arrive, send, max(extra), count, deepest


ARRIVE, SEND, SLOTS, SENDS, DEPTH = programs()
PARTS = 4
OFFSET = tuple(2 * d for d in range(DEPTH + 1))


def kernel(heads, group, blk_count,
           docs, q_hbm, k_hbm, v_hbm, o_hbm,
           window, q_all, o_all, bias,
           own_sem, q_sem, o_sem, send_sem, recv_sem):
    blk, half = lax.axis_index("blk"), lax.axis_index("head")
    me = jnp.where(half == 0, blk, BLOCKS - 1 - blk)
    z_hi, x, y = blk // 16, lax.rem(blk // 4, 4), lax.rem(blk, 4)

    def own_copy(u, h):
        cols = pl.ds(pl.multiple_of(h * D, D), D)
        return pltpu.make_async_copy(
            (k_hbm, v_hbm)[u].at[:, cols], window.at[h, 0, u], own_sem.at[u, h])

    def q_copy(h):
        cols = pl.ds(pl.multiple_of(h * group * D, group * D), group * D)
        return pltpu.make_async_copy(q_hbm.at[:, cols], q_all.at[h], q_sem.at[h])

    def o_copy(h):
        cols = pl.ds(pl.multiple_of(h * group * D, group * D), group * D)
        return pltpu.make_async_copy(o_all.at[h], o_hbm.at[:, cols], o_sem.at[h])

    def hop(h, s_slot, d_slot, there, depth):
        early = there < BLOCKS // 2
        return pltpu.make_async_remote_copy(
            src_ref=window.at[h, s_slot], dst_ref=window.at[h, d_slot],
            send_sem=send_sem.at[0], recv_sem=recv_sem.at[h, depth - 1],
            device_id={"blk": there if early else BLOCKS - 1 - there, "head": 0 if early else 1},
            device_id_type=MESH)

    def wait_bytes(ref, sem):
        pltpu.make_async_copy(ref, ref, sem).wait()

    def on_block(body, low=0, high=BLOCKS):
        if high - low == 1:
            return body(low)
        mid = (low + high) // 2

        @pl.when(me < mid)
        def _():
            on_block(body, low, mid)

        @pl.when(me >= mid)
        def _():
            on_block(body, mid, high)

    barrier = pltpu.get_barrier_semaphore()
    for dx, dy, dz in [tuple(hops * (axis == at) for at in range(3))
                       for axis in range(3) for hops in (1, 2, 3)]:
        z = lax.rem(2 * z_hi + half + dz, 4)
        there = {"blk": z // 2 * 16 + lax.rem(x + dx, 4) * 4 + lax.rem(y + dy, 4),
                 "head": lax.rem(z, 2)}
        pl.semaphore_signal(barrier, inc=1, device_id=there, device_id_type=MESH)

    @pl.loop(0, heads)
    def _(h):
        for u in range(2):
            own_copy(u, h).start()

    my_doc = docs[me]
    for slot in range(SPAN):
        at = me - slot
        same = (at >= 0) & (docs[jnp.maximum(at, 0)] == my_doc)
        bias[slot * T:(slot + 1) * T] = jnp.where(
            lax.broadcasted_iota(jnp.int32, (T, D), 1) == 0,
            jnp.where(same, 0.0, -1e30), 0.0).astype(jnp.bfloat16)

        @pl.when(at < 0)
        def _(slot=slot):
            @pl.loop(0, heads)
            def _(h):
                window[h, slot] = jnp.zeros((2, T, D), jnp.bfloat16)

    pl.semaphore_wait(barrier, 9)

    lane = lax.broadcasted_iota(jnp.int32, (1, D), 1)
    factor = math.log2(math.e) / math.sqrt(D)

    def attend(h, part, parts):
        count = group // parts
        first = part * count
        key = jnp.concatenate([window[h, :SPAN, 0].reshape(SPAN * T, D), bias[...]], axis=1)
        value = jnp.concatenate(
            [window[h, :SPAN, 1].reshape(SPAN * T, D),
             jnp.ones((SPAN * T, D), jnp.bfloat16)], axis=1)
        marker = jnp.broadcast_to(jnp.where(lane == 0, 1.0, 0.0), (count * T, D))
        query = jnp.concatenate(
            [jnp.concatenate([q_all[h, :, (first + g) * D:(first + g + 1) * D]
                              for g in range(count)], axis=0), marker.astype(jnp.bfloat16)], axis=1)
        row = lax.broadcasted_iota(jnp.int32, (1, T, T), 1)
        column = lax.broadcasted_iota(jnp.int32, (1, T, T), 2)
        causal = jnp.broadcast_to(column <= row, (count, T, T)).reshape(count * T, T)
        score = lax.dot_general(query, key, (((1,), (1,)), ((), ())),
                                preferred_element_type=jnp.float32)
        pieces = [jnp.where(causal, score[:, :T], -1e30)]
        pieces += [score[:, n * T:(n + 1) * T] for n in range(1, SPAN)]
        top = jnp.max(functools.reduce(jnp.maximum, pieces), axis=1, keepdims=True)
        weight = jnp.concatenate(
            [jnp.exp2((piece - top) * factor).astype(jnp.bfloat16) for piece in pieces], axis=1)
        summed = jnp.dot(weight, value, preferred_element_type=jnp.float32)
        out = (summed[:, :D] / summed[:, D:]).astype(jnp.bfloat16)
        for g in range(count):
            o_all[h, :, (first + g) * D:(first + g + 1) * D] = out[g * T:(g + 1) * T]

    @pl.loop(0, heads + OFFSET[DEPTH])
    def _(i):
        @pl.when(i < heads)
        def _():
            q_copy(i).start()
            for u in range(2):
                own_copy(u, i).wait()

        def travel(block):
            for depth in range(DEPTH, -1, -1):
                h = i - OFFSET[depth]
                slots = ARRIVE[block].get(depth, []) if depth else [0]
                if not slots:
                    continue

                @pl.when((h >= 0) & (h < heads))
                def _(h=h, slots=slots, depth=depth):
                    if depth:
                        wait_bytes(window.at[h, pl.ds(0, len(slots))], recv_sem.at[h, depth - 1])
                    for slot in slots:
                        for there, d_slot, later in SEND[block].get(slot, ()):
                            hop(h, slot, d_slot, there, later).start()

        on_block(travel)
        done = i - OFFSET[DEPTH]

        @pl.when(done >= 0)
        def _():
            q_copy(done).wait()
            for part in range(PARTS):
                attend(done, part, PARTS)

            o_copy(done).start()

    def finish(block):
        if SENDS[block]:
            wait_bytes(window.at[:, pl.ds(0, SENDS[block])], send_sem.at[0])

    on_block(finish)

    @pl.loop(0, heads)
    def _(h):
        o_copy(h).wait()


def on_device(queries, keys, values, block_docs):
    blk_count = lax.axis_size("blk")
    heads = keys.shape[1] // D
    group = queries.shape[1] // keys.shape[1]
    anywhere = pl.BlockSpec(memory_space=pltpu.HBM)
    return pl.pallas_call(
        functools.partial(kernel, heads, group, blk_count),
        out_shape=jax.ShapeDtypeStruct(queries.shape, jnp.bfloat16),
        in_specs=[pl.BlockSpec(memory_space=pltpu.SMEM), anywhere, anywhere, anywhere],
        out_specs=anywhere,
        scratch_shapes=[
            pltpu.VMEM((heads, SLOTS, 2, T, D), jnp.bfloat16),
            pltpu.VMEM((heads, T, group * D), jnp.bfloat16),
            pltpu.VMEM((heads, T, group * D), jnp.bfloat16),
            pltpu.VMEM((SPAN * T, D), jnp.bfloat16),
            pltpu.SemaphoreType.DMA((2, heads)),
            pltpu.SemaphoreType.DMA((heads,)),
            pltpu.SemaphoreType.DMA((heads,)),
            pltpu.SemaphoreType.DMA((1,)),
            pltpu.SemaphoreType.DMA((heads, DEPTH)),
        ],
        compiler_params=pltpu.CompilerParams(
            collective_id=0, has_side_effects=True, vmem_limit_bytes=62 << 20),
        name="window_attention",
    )(block_docs, queries, keys, values)


def solution(mesh):
    rows = P(("dp", "blk", "head"), None)
    return jax.shard_map(
        on_device, mesh=mesh, in_specs=(rows, rows, rows, P("dp")), out_specs=rows,
        check_vma=False)
```

time: 57.2 us -> 52.6 us (0.920)
  the two profiles are of different devices: /device:TPU:0 before, /device:TPU:64 now
where the time goes in v3:
time: 52.6 us; the launch traced here: 52.4 us
  Pallas kernels  49.3 us (94%)
  local copies, waits for them, and re-layouts  3.1 us (6%)
    pallas_call x1, Pallas kernels, on_device(): pl.pallas_call(functools.partial(kernel, heads, group, blk_count), out_sh...  49.3 us
    unnamed x1, local copies, waits for them, and re-layouts  3.1 us

profile of v3, /device:TPU:64, one launch (start us, length us, event | category | flops | bytes accessed | tf_op | source)
XLA Modules:
  0.0 52.4 jit_solution(3680068838707761687)
XLA Ops:
  0.0 49.3 %window_attention.1 = bf16[128,8192]{1,0:T(8,128)(2,1)} custom-call(s32[64]{0:T(128)} %docs.1, bf16[128,8192]{1,0:T(8,128)(2,1)} %q_hbm.1, bf16[128,1024]{1,0:T(8,128)(2,1)} %k_hbm.1, bf16[128,1024]{1,0:T(8,128)(2,1)} %v_hbm.1), custom_call_target="tpu_custom_call" | custom-call | tf_op jit(solution)/shard_map/window_attention/pallas_call | solution.py:264
  49.3 3.1 %copy.6 = bf16[128,8192]{1,0:T(8,128)(2,1)} copy(bf16[128,8192]{1,0:T(8,128)(2,1)} %window_attention.1) | data formatting | bytes 4194304

commit v4 on v3

--- a/solution.py
+++ b/solution.py
@@ -211,6 +211,10 @@
         for g in range(count):
             o_all[h, :, (first + g) * D:(first + g + 1) * D] = out[g * T:(g + 1) * T]
 
+    ready = jnp.int32(0)
+    for block in range(BLOCKS):
+        ready = jnp.where(me == block, OFFSET[max(ARRIVE[block], default=0)], ready)
+
     @pl.loop(0, heads + OFFSET[DEPTH])
     def _(i):
         @pl.when(i < heads)
@@ -235,9 +239,9 @@
                             hop(h, slot, d_slot, there, later).start()
 
         on_block(travel)
-        done = i - OFFSET[DEPTH]
-
-        @pl.when(done >= 0)
+        done = i - ready
+
+        @pl.when((done >= 0) & (done < heads))
         def _():
             q_copy(done).wait()
             for part in range(PARTS):

time: 52.6 us -> 53.5 us (1.017)
  Pallas kernels: 49.3 us -> 50.3 us
    pallas_call x1, Pallas kernels: 49.3 us -> 50.3 us  [on_device(): pl.pallas_call(functools.partial(kernel, heads, group, blk_count), out_sh...]
where the time goes in v4:
time: 53.5 us; the launch traced here: 53.4 us
  Pallas kernels  50.3 us (94%)
  local copies, waits for them, and re-layouts  3.1 us (6%)
    pallas_call x1, Pallas kernels, on_device(): pl.pallas_call(functools.partial(kernel, heads, group, blk_count), out_sh...  50.3 us
    unnamed x1, local copies, waits for them, and re-layouts  3.1 us

profile of v4, /device:TPU:64, one launch (start us, length us, event | category | flops | bytes accessed | tf_op | source)
XLA Modules:
  0.0 53.4 jit_solution(842172400137732410)
XLA Ops:
  0.0 50.3 %window_attention.1 = bf16[128,8192]{1,0:T(8,128)(2,1)} custom-call(s32[64]{0:T(128)} %docs.1, bf16[128,8192]{1,0:T(8,128)(2,1)} %q_hbm.1, bf16[128,1024]{1,0:T(8,128)(2,1)} %k_hbm.1, bf16[128,1024]{1,0:T(8,128)(2,1)} %v_hbm.1), custom_call_target="tpu_custom_call" | custom-call | tf_op jit(solution)/shard_map/window_attention/pallas_call | solution.py:268
  50.3 3.1 %copy.6 = bf16[128,8192]{1,0:T(8,128)(2,1)} copy(bf16[128,8192]{1,0:T(8,128)(2,1)} %window_attention.1) | data formatting | bytes 4194304
